TPU v7x, 32 devices: a whole 2x2x4 slice. The times are simulated.
32 devices in a mesh: groups: 2 (over y), docs: 8 (over z, x), help: 2 (over core).
Axes of the slice: x: 2, y: 2, z: 4, core: 2. Of those that a mesh axis runs over, the one named last changes fastest.
Arguments:
- token_states: bfloat16 [4096, 2, 1024], P(('groups', 'docs', 'help')), parts along dimension 0, may hold values from -6 to 6
- lengths: int32 [4096], P(('groups', 'docs', 'help')), parts along dimension 0, may hold values from 1 to 2
- cluster_id: int32 [4096], P(('groups', 'docs', 'help')), parts along dimension 0, may hold values from 0 to 7, as said below
- proj_weight: bfloat16 [1024, 1024], replicated, may hold values from -0.1875 to 0.1875
- proj_bias: float32 [1024], replicated, may hold values from -4 to 4
Outputs:
- max_sim: float32 [4096], P(('groups', 'docs', 'help')), parts along dimension 0
There are 2 independent parts, one for each index of `groups`. A program takes and returns all parts, laid end to end along the dimension named above; an argument that names none is the same for every part. Nothing has to cross between parts.
Inputs may be any that keep to these rules, and one draw needn't show every extreme that they name: `cluster_id`: clusters 1 * k to 1 * k + 1 - 1 form owner k. Among the 128 documents of one device (aligned blocks of the document dimension), at most 32 belong to one owner, and in every draw one owner gets exactly 32 documents from every device.
All inputs are finite; a program needn't handle non-finite values.
Results may differ from a plain program's by a relative error of at most 0.0003.
Values may be sent and summed in bfloat16 or wider, within the bound.
A program may use at most 64 MiB of HBM per device.

v0:
```python
import jax
import jax.numpy as jnp
from jax import lax
from jax.sharding import PartitionSpec as P

CL_OWN = 1


def partner(value, axis, bit):
    return lax.ppermute(value, axis, [(i, i ^ 1 << bit) for i in range(lax.axis_size(axis))])


def slot_maxima(own_emb, own_ids, self_pos, col_emb, col_ids):
    row_total = own_emb.shape[0]
    block = min(row_total, 512)
    col_pos = lax.broadcasted_iota(jnp.int32, (col_emb.shape[0],), 0)

    def block_max(pieces):
        part_emb, part_ids, part_self = pieces
        duplicate_scores = jnp.einsum(
            "rd,cd->rc", part_emb, col_emb, preferred_element_type=jnp.float32
        )
        match = (
            (part_ids[:, None] == col_ids[None, :])
            & (col_ids[None, :] >= 0)
            & (part_self[:, None] != col_pos[None, :])
        )
        return jnp.max(jnp.where(match, duplicate_scores, -1.0), axis=1)

    steps_count = row_total // block
    result = lax.map(
        block_max,
        (
            own_emb.reshape(steps_count, block, own_emb.shape[1]),
            own_ids.reshape(steps_count, block),
            self_pos.reshape(steps_count, block),
        ),
    )
    return result.reshape(row_total)


def body(token_states, lengths, cluster_id, proj_weight, proj_bias):
    row_count, seq_len, feat_dim = token_states.shape
    owners = lax.axis_size("docs")
    slot_cap = 2 * row_count // owners
    position_count = owners * slot_cap
    token_mask = (
        lax.broadcasted_iota(jnp.int32, (row_count, seq_len), 1) < lengths[:, None]
    ).astype(jnp.bfloat16)
    summed = jnp.einsum("rsd,rs->rd", token_states, token_mask, preferred_element_type=jnp.float32)
    pooled = (summed / lengths[:, None].astype(jnp.float32)).astype(jnp.bfloat16)
    hidden = jnp.tanh(jnp.dot(pooled, proj_weight, preferred_element_type=jnp.float32) + proj_bias)
    factor = lax.rsqrt(jnp.sum(hidden * hidden, axis=1, keepdims=True) + 1e-06)
    embedded = (hidden * factor).astype(jnp.bfloat16)
    dest_owner = cluster_id // CL_OWN
    same_owner = dest_owner[:, None] == dest_owner[None, :]
    earlier = lax.broadcasted_iota(jnp.int32, (row_count, row_count), 1) < lax.broadcasted_iota(
        jnp.int32, (row_count, row_count), 0
    )
    slot_rank = jnp.sum((same_owner & earlier).astype(jnp.int32), axis=1)
    target = dest_owner * slot_cap + slot_rank
    chooser = lax.broadcasted_iota(jnp.int32, (position_count, row_count), 0) == target[None, :]
    packed = jnp.dot(
        chooser.astype(jnp.bfloat16), embedded, preferred_element_type=jnp.float32
    ).astype(jnp.bfloat16)
    packed_ids = jnp.max(jnp.where(chooser, cluster_id[None, :], -1), axis=1)
    own_emb, own_ids = (
        lax.all_to_all(packed, "docs", split_axis=0, concat_axis=0, tiled=True),
        lax.all_to_all(packed_ids, "docs", split_axis=0, concat_axis=0, tiled=True),
    )
    mate_emb, mate_ids = partner((own_emb, own_ids), "help", 0)
    col_emb = jnp.concatenate([own_emb, mate_emb], axis=0)
    col_ids = jnp.concatenate([own_ids, mate_ids], axis=0)
    self_pos = lax.broadcasted_iota(jnp.int32, (position_count,), 0)
    maxima = slot_maxima(own_emb, own_ids, self_pos, col_emb, col_ids)
    returned = lax.all_to_all(maxima, "docs", split_axis=0, concat_axis=0, tiled=True)
    return jnp.max(jnp.where(chooser, returned[:, None], -3.0), axis=0)


def solution(mesh):
    in_specs = (
        P(("groups", "docs", "help"), None, None),
        P(("groups", "docs", "help")),
        P(("groups", "docs", "help")),
        P(),
        P(),
    )
    out_specs = P(("groups", "docs", "help"))
    return jax.shard_map(body, mesh=mesh, in_specs=in_specs, out_specs=out_specs, check_vma=False)
```

profile of v0, /device:TPU:0, one launch (start us, length us, event | category | flops | bytes accessed | tf_op | source)
XLA Modules:
  0.0 52.2 jit_solution(1633893404897580692)
XLA Ops:
  0.0 0.0 copy-start
  0.0 0.0 copy-start.2
  0.0 0.9 %fusion.14 = pred[128,2,1]{1,0,2:T(32,128)(4,1)S(1)} fusion(s32[128]{0:T(128)} %param.6), kind=kLoop, calls=%fused_computation.26 | loop fusion | flops 256 | bytes 768 | tf_op jit(solution)/shard_map/lt | solution.py:48
  0.9 0.7 %convert_element_type.19 = f32[128]{0:T(128)S(1)} convert(s32[128]{0:T(128)} %param.6) | non-fusion elementwise | flops 128 | bytes 1024 | tf_op jit(solution)/shard_map/convert_element_type | solution.py:51
  1.6 0.9 %convert_reduce_fusion = s32[128]{0:T(128)S(1)} fusion(s32[128]{0:T(128)} %param.7), kind=kLoop, calls=%fused_computation.23 | loop fusion | flops 81792 | bytes 1024 | tf_op jit(solution)/shard_map/reduce_sum | solution.py:60
  2.5 0.7 %multiply_add_fusion = s32[128]{0:T(128)S(1)} fusion(s32[128]{0:T(128)S(1)} %convert_reduce_fusion, s32[128]{0:T(128)} %param.7), kind=kLoop, calls=%fused_computation.31 | loop fusion | flops 256 | bytes 1536 | tf_op jit(solution)/shard_map/add | solution.py:61
  3.1 1.7 %fusion.10 = f32[128,1,1024]{2,1,0:T(1,128)S(1)} fusion(bf16[128,2,1024]{2,1,0:T(2,128)(2,1)} %param.5, pred[128,2,1]{1,0,2:T(32,128)(4,1)S(1)} %fusion.14), kind=kOutput, calls=%fused_computation.16 | convolution fusion | flops 524288 | bytes 1048832 | tf_op jit(solution)/shard_map/rsd,rs->rd/dot_general | solution.py:50
  4.9 0.0 copy-done
  4.9 0.0 copy-done.2
  4.9 0.6 %multiply_reduce_fusion = (f32[128]{0:T(128)S(1)}, f32[128,1024]{1,0:T(8,128)S(1)}) fusion(f32[1024]{0:T(1024)S(1)} %copy-done.2, bf16[1024,1024]{1,0:T(8,128)(2,1)S(1)} %copy-done, f32[128,1,1024]{2,1,0:T(1,128)S(1)} %fusion.10, f32[128]{0:T(128)S(1)} %convert_element_type.19), kind=kOutput, calls=%fused_computation.11 | convolution fusion | flops 269090688 | bytes 3150848 | tf_op jit(solution)/shard_map/dot_general | solution.py:52
  5.5 0.0 copy-start.1
  5.5 0.4 convolution_convert_fusion
  5.9 21.6 %all_to_all.30 = bf16[8,32,1024]{2,1,0:T(8,128)(2,1)S(1)} all-to-all(bf16[8,32,1024]{2,1,0:T(8,128)(2,1)S(1)} %bitcast.18), channel_id=1, replica_groups=mesh['groups'=2,'docs'=8,'help'=2] {'docs'}, dimensions={0} | all-to-all | bytes 1048576 | tf_op jit(solution)/shard_map/all_to_all | solution.py:68
  27.5 0.0 collective-permute-start.1
  27.5 0.0 copy-done.1
  27.5 0.1 select_reduce_fusion.2
  27.6 0.7 %all_to_all.20 = s32[8,32,1]{1,0,2:T(8,128)} reshape(s32[256]{0:T(256)S(1)} %select_reduce_fusion.2) | data formatting | bytes 2048 | tf_op jit(solution)/shard_map/all_to_all | solution.py:69
  28.3 3.6 %all-to-all-start = ((s32[8,32,1]{1,2,0:T(1,128)}), s32[8,32,1]{1,2,0:T(1,128)S(1)}, u32[]{:S(2)}, u32[]{:S(2)}) async-start(s32[8,32,1]{1,2,0:T(1,128)} %bitcast), calls=%async_computation | async-start | bytes 8192 | tf_op jit(solution)/shard_map/all_to_all | solution.py:69
  31.9 6.5 %all-to-all-done = s32[8,32,1]{1,2,0:T(1,128)S(1)} async-done(((s32[8,32,1]{1,2,0:T(1,128)}), s32[8,32,1]{1,2,0:T(1,128)S(1)}, u32[]{:S(2)}, u32[]{:S(2)}) %all-to-all-start) | async-done | bytes 1056 | tf_op jit(solution)/shard_map/all_to_all | solution.py:69
  38.4 0.5 broadcast.36
  38.9 0.7 %reduce.6 = s32[8,32]{1,0:T(8,128)S(1)} reduce(s32[8,32,1]{1,2,0:T(1,128)S(1)} %all-to-all-done, s32[]{:T(128)} %broadcast.36), dimensions={2}, to_apply=%all_to_all.21.reduce_sub_computation.3 | reduce | bytes 2052 | tf_op jit(solution)/shard_map/all_to_all | solution.py:69
  39.5 0.1 eq.48
  39.6 0.0 collective-permute-start
  39.6 1.1 %collective-permute-done = s32[256]{0:T(256)S(1)} collective-permute-done((s32[256]{0:T(256)S(1)}, s32[256]{0:T(256)S(1)}, u32[]{:S(2)}, u32[]{:S(2)}) %collective-permute-start) | collective-permute-done | bytes 1056 | tf_op jit(solution)/shard_map/ppermute | solution.py:10
  40.8 0.0 collective-permute-done.1
  40.8 0.6 %select_reduce_fusion = f32[256]{0:T(256)S(1)} fusion(s32[512]{0:T(512)S(1)} %constant_dynamic-update-slice_fusion, s32[256]{0:T(256)S(1)} %eq.48, pred[512]{0:T(512)(128)(4,1)S(1)} %broadcast_compare_fusion, bf16[256,1024]{1,0:T(8,128)(2,1)S(1)} %bitcast.20, bf16[256,1024]{1,0:T(8,128)(2,1)S(1)} %collective-permute-done.1), kind=kOutput, calls=%fused_computation.9 | convolution fusion | flops 271318784 | bytes 1053184 | tf_op jit(solution)/shard_map/while/body/eval_jaxpr/rd,cd->rc/dot_general | solution.py:20
  41.4 0.1 all_to_all.25
  41.5 8.9 %all_to_all.31 = f32[8,32,1]{1,2,0:T(1,128)S(1)} all-to-all(f32[8,32,1]{1,2,0:T(1,128)S(1)} %bitcast.21), channel_id=1, replica_groups=mesh['groups'=2,'docs'=8,'help'=2] {'docs'}, dimensions={0} | all-to-all | bytes 2048 | tf_op jit(solution)/shard_map/all_to_all | solution.py:76
  50.3 0.5 broadcast.37
  50.8 0.7 %reduce.7 = f32[8,32]{1,0:T(8,128)S(1)} reduce(f32[8,32,1]{1,2,0:T(1,128)S(1)} %all_to_all.31, f32[]{:T(128)} %broadcast.37), dimensions={2}, to_apply=%all_to_all.26.reduce_sub_computation.3 | reduce | bytes 2052 | tf_op jit(solution)/shard_map/all_to_all | solution.py:76
  51.5 0.1 broadcast_in_dim.56
  51.6 0.6 %select_reduce_fusion.1 = f32[128]{0:T(128)} fusion(f32[256]{0:T(256)S(1)} %broadcast_in_dim.56, s32[128]{0:T(128)S(1)} %multiply_add_fusion), kind=kLoop, calls=%fused_computation.18 | loop fusion | flops 98176 | bytes 2048 | tf_op jit(solution)/shard_map/reduce_max | solution.py:77
  (5 shorter events, 0.0 us)
Async XLA Ops:
  0.0 4.9 %copy-start = (bf16[1024,1024]{1,0:T(8,128)(2,1)S(1)}, bf16[1024,1024]{1,0:T(8,128)(2,1)}, u32[]{:S(2)}) copy-start(bf16[1024,1024]{1,0:T(8,128)(2,1)} %param.8) | copy-start | bytes 6291460
  0.0 4.9 %copy-start.2 = (f32[1024]{0:T(1024)S(1)}, f32[1024]{0:T(1024)}, u32[]{:S(2)}) copy-start(f32[1024]{0:T(1024)} %param.9) | copy-start | bytes 12292
  5.5 22.0 %copy-start.1 = (s32[128]{0:T(128)S(1)}, s32[128]{0:T(128)}, u32[]{:S(2)}) copy-start(s32[128]{0:T(128)} %param.7) | copy-start | bytes 1540
  27.5 13.3 %collective-permute-start.1 = (bf16[256,1024]{1,0:T(8,128)(2,1)S(1)}, bf16[256,1024]{1,0:T(8,128)(2,1)S(1)}, u32[]{:S(2)}, u32[]{:S(2)}) collective-permute-start(bf16[256,1024]{1,0:T(8,128)(2,1)S(1)} %bitcast.19), channel_id=1, source_target_pairs={{0,1},{1,0},{2,3},{3,2},{4,5},{5,4},{6,7},{7,6},{8,9},{9,8},{10,11... | collective-permute-start | bytes 1572872 | tf_op jit(solution)/shard_map/ppermute | solution.py:10
  28.3 10.1 %all-to-all-start = ((s32[8,32,1]{1,2,0:T(1,128)}), s32[8,32,1]{1,2,0:T(1,128)S(1)}, u32[]{:S(2)}, u32[]{:S(2)}) async-start(s32[8,32,1]{1,2,0:T(1,128)} %bitcast), calls=%async_computation | async-start | bytes 8192 | tf_op jit(solution)/shard_map/all_to_all | solution.py:69
  39.6 1.2 %collective-permute-start = (s32[256]{0:T(256)S(1)}, s32[256]{0:T(256)S(1)}, u32[]{:S(2)}, u32[]{:S(2)}) collective-permute-start(s32[256]{0:T(256)S(1)} %eq.48), channel_id=1, source_target_pairs={{0,1},{1,0},{2,3},{3,2},{4,5},{5,4},{6,7},{7,6},{8,9},{9,8},{10,11... | collective-permute-start | bytes 3080 | tf_op jit(solution)/shard_map/ppermute | solution.py:10
where the time goes:
time: 52.5 us; the launch traced here: 52.2 us
  blocking collectives  30.5 us (58%)
  waiting for transfers between devices  7.63 us (15%)
  other arithmetic  5.19 us (10%)
  starting transfers between devices  3.61 us (7%)
  matrix products  3.24 us (6%)
  local copies, waits for them, and re-layouts  1.97 us (4%)
    all_to_all x1, blocking collectives, body(): lax.all_to_all(packed, 'docs', split_axis=0, concat_axis=0, tiled=True)  21.6 us
    all_to_all x1, blocking collectives, body(): lax.all_to_all(maxima, 'docs', split_axis=0, concat_axis=0, tiled=True)  8.85 us
    all_to_all x1, waiting for transfers between devices, body(): lax.all_to_all(packed_ids, 'docs', split_axis=0, concat_axis=0, tiled=True)  6.49 us
    all_to_all x1, starting transfers between devices, body(): lax.all_to_all(packed_ids, 'docs', split_axis=0, concat_axis=0, tiled=True)  3.6 us
    dot_general x1, matrix products, body(): jnp.einsum('rsd,rs->rd', token_states, token_mask, preferred_element_type...  1.73 us
    all_to_all x2, local copies, waits for them, and re-layouts, body(): lax.all_to_all(packed_ids, 'docs', split_axis=0, concat_axis=0, tiled=True)  1.19 us
    ppermute x2, waiting for transfers between devices, partner(): lax.ppermute(value, axis, [(i, i ^ 1 << bit) for i in range(lax.axis_size...  1.14 us
  transfers between devices with their start and end apart: 3, of which 2 were waited for; matrix products, arithmetic and copies ran while one was open for 3% of the time, Pallas kernels for 0%

commit v1 on v0

--- a/solution.py
+++ b/solution.py
@@ -1,6 +1,10 @@
+import functools
+
 import jax
 import jax.numpy as jnp
 from jax import lax
+from jax.experimental import pallas as pl
+from jax.experimental.pallas import tpu as pltpu
 from jax.sharding import PartitionSpec as P
 
 CL_OWN = 1
@@ -77,6 +81,207 @@
     return jnp.max(jnp.where(chooser, returned[:, None], -3.0), axis=0)
 
 
+EMPTY = 2.0
+DIRECT_LIMIT = 16
+
+
+def flipped(index, step):
+    bit = 1
+    while bit <= step:
+        if step & bit:
+            index = index + bit * (1 - 2 * ((index // bit) % 2))
+        bit *= 2
+    return index
+
+
+def send_order(owners):
+    half = owners // 2
+    return list(range(half, owners)) + list(range(half - 1, 0, -1))
+
+
+def fused_kernel(
+    owners,
+    slot_cap,
+    pooled_ref,
+    ids_ref,
+    weight_hbm,
+    bias_ref,
+    out_ref,
+    weight_ref,
+    packed_ref,
+    own_ref,
+    mate_ref,
+    maxima_ref,
+    returned_ref,
+    weight_sem,
+    pack_send,
+    pack_recv,
+    mate_send,
+    mate_recv,
+    back_send,
+    back_recv,
+):
+    me = lax.axis_index("docs")
+    side = lax.axis_index("help")
+    mate = {"help": 1 - side}
+    order = send_order(owners)
+    positions = owners * slot_cap
+    row_count, feat_dim = pooled_ref.shape
+
+    weight_copy = pltpu.make_async_copy(weight_hbm, weight_ref, weight_sem)
+    weight_copy.start()
+    barrier = pltpu.get_barrier_semaphore()
+    for step in order:
+        pl.semaphore_signal(
+            barrier, inc=1, device_id={"docs": flipped(me, step)}, device_id_type=pl.DeviceIdType.MESH
+        )
+    pl.semaphore_signal(barrier, inc=1, device_id=mate, device_id_type=pl.DeviceIdType.MESH)
+
+    ids = ids_ref[...]
+    across = jnp.broadcast_to(ids, (row_count, row_count))
+    down = jnp.transpose(across)
+    earlier = lax.broadcasted_iota(jnp.int32, (row_count, row_count), 0) < lax.broadcasted_iota(
+        jnp.int32, (row_count, row_count), 1
+    )
+    rank = jnp.sum(jnp.where((across == down) & earlier, 1, 0), axis=0, keepdims=True)
+    target = jnp.bitwise_xor(ids // CL_OWN, me) * slot_cap + rank
+
+    weight_copy.wait()
+    hidden = jnp.tanh(
+        jnp.dot(pooled_ref[...], weight_ref[...], preferred_element_type=jnp.float32) + bias_ref[...]
+    )
+    factor = lax.rsqrt(jnp.sum(hidden * hidden, axis=1, keepdims=True) + 1e-06)
+    embedded = (hidden * factor).astype(jnp.bfloat16)
+
+    def pack(step):
+        slots = lax.broadcasted_iota(jnp.int32, (slot_cap, row_count), 0) + step * slot_cap
+        chooser = jnp.where(slots == target, 1.0, 0.0)
+        filled = jnp.sum(chooser, axis=1, keepdims=True)
+        rows = jnp.dot(
+            chooser.astype(jnp.bfloat16), embedded, preferred_element_type=jnp.float32
+        )
+        return jnp.where(filled > 0.5, rows, EMPTY).astype(jnp.bfloat16)
+
+    def to_owner(step):
+        return pltpu.make_async_remote_copy(
+            src_ref=packed_ref.at[step],
+            dst_ref=own_ref.at[step],
+            send_sem=pack_send.at[step],
+            recv_sem=pack_recv.at[step],
+            device_id={"docs": flipped(me, step)},
+            device_id_type=pl.DeviceIdType.MESH,
+        )
+
+    def to_mate(step):
+        return pltpu.make_async_remote_copy(
+            src_ref=own_ref.at[step],
+            dst_ref=mate_ref.at[step],
+            send_sem=mate_send.at[step],
+            recv_sem=mate_recv.at[step],
+            device_id=mate,
+            device_id_type=pl.DeviceIdType.MESH,
+        )
+
+    def to_source(step):
+        return pltpu.make_async_remote_copy(
+            src_ref=maxima_ref,
+            dst_ref=returned_ref.at[step],
+            send_sem=back_send.at[step],
+            recv_sem=back_recv.at[step],
+            device_id={"docs": flipped(me, step)},
+            device_id_type=pl.DeviceIdType.MESH,
+        )
+
+    packed_ref[order[0]] = pack(order[0])
+    pl.semaphore_wait(barrier, owners)
+    to_owner(order[0]).start()
+    for step in order[1:]:
+        packed_ref[step] = pack(step)
+        to_owner(step).start()
+    own_ref[0] = pack(0)
+    to_mate(0).start()
+    for step in reversed(order):
+        to_owner(step).wait_recv()
+        to_mate(step).start()
+    for step in range(owners):
+        to_mate(step).wait_recv()
+
+    own = own_ref[...].reshape(positions, feat_dim)
+
+    def column_max(columns, exclude_self):
+        scores = lax.dot_general(
+            columns, own, (((1,), (1,)), ((), ())), preferred_element_type=jnp.float32
+        )
+        keep = columns[:, 0:1].astype(jnp.float32) < 1.5
+        if exclude_self:
+            keep = keep & (
+                lax.broadcasted_iota(jnp.int32, (positions, positions), 0)
+                != lax.broadcasted_iota(jnp.int32, (positions, positions), 1)
+            )
+        return jnp.max(jnp.where(keep, scores, -1.0), axis=0, keepdims=True)
+
+    maxima = jnp.maximum(
+        column_max(own, True), column_max(mate_ref[...].reshape(positions, feat_dim), False)
+    )
+    maxima_ref[...] = maxima
+    for step in order:
+        to_source(step).start()
+
+    place = lax.broadcasted_iota(jnp.int32, (1, positions), 1) // slot_cap
+    merged = jnp.where(place == 0, maxima, 0.0)
+    for step in order:
+        to_source(step).wait_recv()
+        merged = jnp.where(place == step, returned_ref[step], merged)
+    finder = jnp.where(
+        lax.broadcasted_iota(jnp.int32, (positions, row_count), 0) == target, 1.0, 0.0
+    )
+    picked = jnp.dot(
+        jnp.broadcast_to(merged, (8, positions)),
+        finder,
+        preferred_element_type=jnp.float32,
+        precision=lax.Precision.HIGHEST,
+    )
+    out_ref[...] = jnp.maximum(picked[0:1], -1.0)
+    for step in order:
+        to_owner(step).wait_send()
+        to_source(step).wait_send()
+    for step in range(owners):
+        to_mate(step).wait_send()
+
+
+def fused_body(token_states, lengths, cluster_id, proj_weight, proj_bias):
+    row_count, seq_len, feat_dim = token_states.shape
+    owners = lax.axis_size("docs")
+    slot_cap = 2 * row_count // owners
+    positions = owners * slot_cap
+    token_mask = (
+        lax.broadcasted_iota(jnp.int32, (row_count, seq_len), 1) < lengths[:, None]
+    ).astype(jnp.float32)
+    summed = jnp.sum(token_states.astype(jnp.float32) * token_mask[:, :, None], axis=1)
+    pooled = (summed / lengths[:, None].astype(jnp.float32)).astype(jnp.bfloat16)
+    vmem = pl.BlockSpec(memory_space=pltpu.VMEM)
+    block = (owners, slot_cap, feat_dim)
+    result = pl.pallas_call(
+        functools.partial(fused_kernel, owners, slot_cap),
+        out_shape=jax.ShapeDtypeStruct((1, row_count), jnp.float32),
+        in_specs=[vmem, vmem, pl.BlockSpec(memory_space=pl.ANY), vmem],
+        out_specs=vmem,
+        scratch_shapes=[
+            pltpu.VMEM(proj_weight.shape, jnp.bfloat16),
+            pltpu.VMEM(block, jnp.bfloat16),
+            pltpu.VMEM(block, jnp.bfloat16),
+            pltpu.VMEM(block, jnp.bfloat16),
+            pltpu.VMEM((1, positions), jnp.float32),
+            pltpu.VMEM((owners, 1, positions), jnp.float32),
+            pltpu.SemaphoreType.DMA,
+        ]
+        + [pltpu.SemaphoreType.DMA((owners,))] * 6,
+        compiler_params=pltpu.CompilerParams(collective_id=0, has_side_effects=True),
+        name="scores",
+    )(pooled, cluster_id[None, :], proj_weight, proj_bias[None, :])
+    return result.reshape(row_count)
+
+
 def solution(mesh):
     in_specs = (
         P(("groups", "docs", "help"), None, None),
@@ -86,4 +291,6 @@
         P(),
     )
     out_specs = P(("groups", "docs", "help"))
-    return jax.shard_map(body, mesh=mesh, in_specs=in_specs, out_specs=out_specs, check_vma=False)
+    owners = mesh.shape["docs"]
+    direct = owners <= DIRECT_LIMIT and owners & (owners - 1) == 0 and mesh.shape["help"] == 2
+    return jax.shard_map(fused_body if direct else body, mesh=mesh, in_specs=in_specs, out_specs=out_specs, check_vma=False)

time: 52.5 us -> 31.2 us (0.59)
  blocking collectives: 30.5 us -> 0 us
  Pallas kernels: 0 us -> 24.9 us
  waiting for transfers between devices: 7.63 us -> 0 us
  starting transfers between devices: 3.61 us -> 0 us
  matrix products: 3.24 us -> 0 us
  local copies, waits for them, and re-layouts: 1.97 us -> 1.18 us
    all_to_all x2 -> x0, blocking collectives: 30.5 us -> none  [the longest x1 21.6 us: body(): lax.all_to_all(packed, 'docs', split_axis=0, concat_axis=0, tiled=True)]
    pallas_call x0 -> x1, Pallas kernels: none -> 24.9 us  [fused_body(): pl.pallas_call(functools.partial(fused_kernel, owners, slot_cap), out_sha...]
    all_to_all x1 -> x0, waiting for transfers between devices: 6.49 us -> none  [body(): lax.all_to_all(packed_ids, 'docs', split_axis=0, concat_axis=0, tiled=True)]
    all_to_all x1 -> x0, starting transfers between devices: 3.6 us -> none  [body(): lax.all_to_all(packed_ids, 'docs', split_axis=0, concat_axis=0, tiled=True)]
    dot_general x4 -> x0, matrix products: 3.24 us -> none  [the longest x1 1.73 us: body(): jnp.einsum('rsd,rs->rd', token_states, token_mask, preferred_element_type...]
    all_to_all x4 -> x0, local copies, waits for them, and re-layouts: 1.78 us -> none  [the longest x2 1.19 us: body(): lax.all_to_all(packed_ids, 'docs', split_axis=0, concat_axis=0, tiled=True)]
    reduce_sum x1, other arithmetic: 0.9 us -> 2.51 us  [fused_body(): jnp.sum(token_states.astype(jnp.float32) * token_mask[:, :, None], axis=1)]
    convert_element_type x1 -> x3, other arithmetic: 0.66 us -> 2.19 us  [the longest x1 0.8 us: fused_body(): (summed / lengths[:, None].astype(jnp.float32)).astype(jnp.bfloat16)]
  transfers between devices with their start and end apart: 3 -> 0, of which waited for: 2 -> 0; matrix products, arithmetic and copies ran while one was open for 3% -> 0% of each run, Pallas kernels for 0% -> 0%
where the time goes in v1:
time: 31.2 us; the launch traced here: 30.8 us
  Pallas kernels  24.9 us (80%)
  other arithmetic  4.7 us (15%)
  local copies, waits for them, and re-layouts  1.18 us (4%)
    pallas_call x1, Pallas kernels, fused_body(): pl.pallas_call(functools.partial(fused_kernel, owners, slot_cap), out_sha...  24.9 us
    reduce_sum x1, other arithmetic, fused_body(): jnp.sum(token_states.astype(jnp.float32) * token_mask[:, :, None], axis=1)  2.51 us
    unnamed x1, local copies, waits for them, and re-layouts  1.18 us
    convert_element_type x1, other arithmetic, fused_body(): (summed / lengths[:, None].astype(jnp.float32)).astype(jnp.bfloat16)  0.8 us
    convert_element_type x1, other arithmetic, fused_body(): token_mask = (lax.broadcasted_iota(jnp.int32, (row_count, seq_len), 1) <...  0.73 us
    convert_element_type x1, other arithmetic, fused_body(): lengths[:, None].astype(jnp.float32)  0.66 us

profile of v1, /device:TPU:0, one launch (start us, length us, event | category | flops | bytes accessed | tf_op | source)
XLA Modules:
  0.0 30.8 jit_solution(17755746362394000563)
XLA Ops:
  0.0 0.7 %convert_element_type.19 = f32[128]{0:T(128)S(1)} convert(s32[128]{0:T(128)} %param.6) | non-fusion elementwise | flops 128 | bytes 1024 | tf_op jit(solution)/shard_map/convert_element_type | solution.py:261
  0.7 0.7 %fusion = f32[128,2]{1,0:T(8,128)S(1)} fusion(s32[128]{0:T(128)} %param.6), kind=kLoop, calls=%fused_computation.3 | loop fusion | flops 512 | bytes 1536 | tf_op jit(solution)/shard_map/convert_element_type | solution.py:259
  1.4 2.5 %multiply_reduce_fusion = f32[128,1024]{1,0:T(8,128)S(1)} fusion(bf16[128,2,1024]{2,1,0:T(2,128)(2,1)} %param.5, f32[128,2]{1,0:T(8,128)S(1)} %fusion), kind=kLoop, calls=%fused_computation | loop fusion | flops 655360 | bytes 1049600 | tf_op jit(solution)/shard_map/reduce_sum | solution.py:260
  3.9 0.8 %divide_convert_fusion.pooled_ref = bf16[128,1024]{1,0:T(8,128)(2,1)} fusion(f32[128,1024]{1,0:T(8,128)S(1)} %multiply_reduce_fusion, f32[128]{0:T(128)S(1)} %convert_element_type.19), kind=kLoop, calls=%fused_computation.1 | loop fusion | flops 262144 | bytes 786944 | tf_op jit(solution)/shard_map/convert_element_type | solution.py:261
  4.7 24.9 %scores.1 = f32[1,128]{1,0:T(1,128)} custom-call(bf16[128,1024]{1,0:T(8,128)(2,1)} %divide_convert_fusion.pooled_ref, s32[1,128]{1,0:T(1,128)} %bitcast.4, bf16[1024,1024]{1,0:T(8,128)(2,1)} %weight_hbm.1, f32[1,1024]{1,0:T(1,128)} %bitcast.3), custom_call_target="tpu_custom_call" | custom-call | tf_op jit(solution)/shard_map/scores/pallas_call | solution.py:264
  29.6 1.2 %copy.7 = f32[128]{0:T(128)} copy(f32[128]{0:T(128)} %bitcast.5) | data formatting | bytes 1024

commit v2 on v1

--- a/solution.py
+++ b/solution.py
@@ -102,7 +102,8 @@
 def fused_kernel(
     owners,
     slot_cap,
-    pooled_ref,
+    states_ref,
+    lengths_ref,
     ids_ref,
     weight_hbm,
     bias_ref,
@@ -126,7 +127,7 @@
     mate = {"help": 1 - side}
     order = send_order(owners)
     positions = owners * slot_cap
-    row_count, feat_dim = pooled_ref.shape
+    row_count, seq_len, feat_dim = states_ref.shape
 
     weight_copy = pltpu.make_async_copy(weight_hbm, weight_ref, weight_sem)
     weight_copy.start()
@@ -146,9 +147,16 @@
     rank = jnp.sum(jnp.where((across == down) & earlier, 1, 0), axis=0, keepdims=True)
     target = jnp.bitwise_xor(ids // CL_OWN, me) * slot_cap + rank
 
+    counts = jnp.transpose(jnp.broadcast_to(lengths_ref[...].astype(jnp.float32), (row_count, row_count)))[:, 0:1]
+    states = states_ref[...]
+    summed = states[:, 0, :].astype(jnp.float32)
+    for position in range(1, seq_len):
+        summed = summed + jnp.where(counts > position, states[:, position, :].astype(jnp.float32), 0.0)
+    pooled = (summed / counts).astype(jnp.bfloat16)
+
     weight_copy.wait()
     hidden = jnp.tanh(
-        jnp.dot(pooled_ref[...], weight_ref[...], preferred_element_type=jnp.float32) + bias_ref[...]
+        jnp.dot(pooled, weight_ref[...], preferred_element_type=jnp.float32) + bias_ref[...]
     )
     factor = lax.rsqrt(jnp.sum(hidden * hidden, axis=1, keepdims=True) + 1e-06)
     embedded = (hidden * factor).astype(jnp.bfloat16)
@@ -254,17 +262,12 @@
     owners = lax.axis_size("docs")
     slot_cap = 2 * row_count // owners
     positions = owners * slot_cap
-    token_mask = (
-        lax.broadcasted_iota(jnp.int32, (row_count, seq_len), 1) < lengths[:, None]
-    ).astype(jnp.float32)
-    summed = jnp.sum(token_states.astype(jnp.float32) * token_mask[:, :, None], axis=1)
-    pooled = (summed / lengths[:, None].astype(jnp.float32)).astype(jnp.bfloat16)
     vmem = pl.BlockSpec(memory_space=pltpu.VMEM)
     block = (owners, slot_cap, feat_dim)
     result = pl.pallas_call(
         functools.partial(fused_kernel, owners, slot_cap),
         out_shape=jax.ShapeDtypeStruct((1, row_count), jnp.float32),
-        in_specs=[vmem, vmem, pl.BlockSpec(memory_space=pl.ANY), vmem],
+        in_specs=[vmem, vmem, vmem, pl.BlockSpec(memory_space=pl.ANY), vmem],
         out_specs=vmem,
         scratch_shapes=[
             pltpu.VMEM(proj_weight.shape, jnp.bfloat16),
@@ -278,7 +281,7 @@
         + [pltpu.SemaphoreType.DMA((owners,))] * 6,
         compiler_params=pltpu.CompilerParams(collective_id=0, has_side_effects=True),
         name="scores",
-    )(pooled, cluster_id[None, :], proj_weight, proj_bias[None, :])
+    )(token_states, lengths[None, :], cluster_id[None, :], proj_weight, proj_bias[None, :])
     return result.reshape(row_count)
 
 

time: 31.2 us -> 26.5 us (0.85)
  other arithmetic: 4.7 us -> 0 us
    reduce_sum x1 -> x0, other arithmetic: 2.51 us -> none  [fused_body(): jnp.sum(token_states.astype(jnp.float32) * token_mask[:, :, None], axis=1)]
    convert_element_type x3 -> x0, other arithmetic: 2.19 us -> none  [the longest x1 0.8 us: fused_body(): (summed / lengths[:, None].astype(jnp.float32)).astype(jnp.bfloat16)]
where the time goes in v2:
time: 26.5 us; the launch traced here: 26.2 us
  Pallas kernels  25 us (94%)
  local copies, waits for them, and re-layouts  1.19 us (4%)
    pallas_call x1, Pallas kernels, fused_body(): pl.pallas_call(functools.partial(fused_kernel, owners, slot_cap), out_sha...  25 us
    unnamed x1, local copies, waits for them, and re-layouts  1.19 us

profile of v2, /device:TPU:0, one launch (start us, length us, event | category | flops | bytes accessed | tf_op | source)
XLA Modules:
  0.0 26.2 jit_solution(805858028030650825)
XLA Ops:
  0.0 25.0 %scores.1 = f32[1,128]{1,0:T(1,128)} custom-call(bf16[128,2,1024]{2,1,0:T(2,128)(2,1)} %states_ref.1, s32[1,128]{1,0:T(1,128)} %bitcast.5, s32[1,128]{1,0:T(1,128)} %bitcast.6, bf16[1024,1024]{1,0:T(8,128)(2,1)} %weight_hbm.1, f32[1,1024]{1,0:T(1,128)} %bitcast.4), custom_call_target="tpu_custom_call" | custom-call | tf_op jit(solution)/shard_map/scores/pallas_call | solution.py:267
  25.0 1.2 %copy.7 = f32[128]{0:T(128)} copy(f32[128]{0:T(128)} %bitcast.7) | data formatting | bytes 1024

commit v3 on v2

v3 whole, which is shorter than its diff:
```python
import functools

import jax
import jax.numpy as jnp
from jax import lax
from jax.experimental import pallas as pl
from jax.experimental.pallas import tpu as pltpu
from jax.sharding import PartitionSpec as P

CL_OWN = 1


def partner(value, axis, bit):
    return lax.ppermute(value, axis, [(i, i ^ 1 << bit) for i in range(lax.axis_size(axis))])


def slot_maxima(own_emb, own_ids, self_pos, col_emb, col_ids):
    row_total = own_emb.shape[0]
    block = min(row_total, 512)
    col_pos = lax.broadcasted_iota(jnp.int32, (col_emb.shape[0],), 0)

    def block_max(pieces):
        part_emb, part_ids, part_self = pieces
        duplicate_scores = jnp.einsum(
            "rd,cd->rc", part_emb, col_emb, preferred_element_type=jnp.float32
        )
        match = (
            (part_ids[:, None] == col_ids[None, :])
            & (col_ids[None, :] >= 0)
            & (part_self[:, None] != col_pos[None, :])
        )
        return jnp.max(jnp.where(match, duplicate_scores, -1.0), axis=1)

    steps_count = row_total // block
    result = lax.map(
        block_max,
        (
            own_emb.reshape(steps_count, block, own_emb.shape[1]),
            own_ids.reshape(steps_count, block),
            self_pos.reshape(steps_count, block),
        ),
    )
    return result.reshape(row_total)


def body(token_states, lengths, cluster_id, proj_weight, proj_bias):
    row_count, seq_len, feat_dim = token_states.shape
    owners = lax.axis_size("docs")
    slot_cap = 2 * row_count // owners
    position_count = owners * slot_cap
    token_mask = (
        lax.broadcasted_iota(jnp.int32, (row_count, seq_len), 1) < lengths[:, None]
    ).astype(jnp.bfloat16)
    summed = jnp.einsum("rsd,rs->rd", token_states, token_mask, preferred_element_type=jnp.float32)
    pooled = (summed / lengths[:, None].astype(jnp.float32)).astype(jnp.bfloat16)
    hidden = jnp.tanh(jnp.dot(pooled, proj_weight, preferred_element_type=jnp.float32) + proj_bias)
    factor = lax.rsqrt(jnp.sum(hidden * hidden, axis=1, keepdims=True) + 1e-06)
    embedded = (hidden * factor).astype(jnp.bfloat16)
    dest_owner = cluster_id // CL_OWN
    same_owner = dest_owner[:, None] == dest_owner[None, :]
    earlier = lax.broadcasted_iota(jnp.int32, (row_count, row_count), 1) < lax.broadcasted_iota(
        jnp.int32, (row_count, row_count), 0
    )
    slot_rank = jnp.sum((same_owner & earlier).astype(jnp.int32), axis=1)
    target = dest_owner * slot_cap + slot_rank
    chooser = lax.broadcasted_iota(jnp.int32, (position_count, row_count), 0) == target[None, :]
    packed = jnp.dot(
        chooser.astype(jnp.bfloat16), embedded, preferred_element_type=jnp.float32
    ).astype(jnp.bfloat16)
    packed_ids = jnp.max(jnp.where(chooser, cluster_id[None, :], -1), axis=1)
    own_emb, own_ids = (
        lax.all_to_all(packed, "docs", split_axis=0, concat_axis=0, tiled=True),
        lax.all_to_all(packed_ids, "docs", split_axis=0, concat_axis=0, tiled=True),
    )
    mate_emb, mate_ids = partner((own_emb, own_ids), "help", 0)
    col_emb = jnp.concatenate([own_emb, mate_emb], axis=0)
    col_ids = jnp.concatenate([own_ids, mate_ids], axis=0)
    self_pos = lax.broadcasted_iota(jnp.int32, (position_count,), 0)
    maxima = slot_maxima(own_emb, own_ids, self_pos, col_emb, col_ids)
    returned = lax.all_to_all(maxima, "docs", split_axis=0, concat_axis=0, tiled=True)
    return jnp.max(jnp.where(chooser, returned[:, None], -3.0), axis=0)


EMPTY = 2.0
DIRECT_LIMIT = 16


def flipped(index, step):
    bit = 1
    while bit <= step:
        if step & bit:
            index = index + bit * (1 - 2 * ((index // bit) % 2))
        bit *= 2
    return index


def fused_kernel(
    owners,
    slot_cap,
    states_hbm,
    lengths_ref,
    ids_ref,
    weight_hbm,
    bias_ref,
    out_ref,
    states_ref,
    weight_ref,
    packed_ref,
    own_ref,
    maxima_ref,
    returned_ref,
    states_sem,
    weight_sem,
    pack_send,
    pack_recv,
    back_send,
    back_recv,
    onward_sem,
):
    me = lax.axis_index("docs")
    side = lax.axis_index("help")
    row_count, seq_len, feat_dim = states_ref.shape
    quarter = owners // 4
    half = owners // 2
    sources = 2 * owners
    late = 2 * 3 * quarter
    group = row_count // slot_cap
    my_half = me // half
    near = me + my_half * (owners - 1 - 2 * me)
    outer = 1 - near // quarter
    is_owner = near >= quarter

    states_copy = pltpu.make_async_copy(states_hbm, states_ref, states_sem)
    states_copy.start()
    weight_copy = pltpu.make_async_copy(weight_hbm, weight_ref, weight_sem)
    weight_copy.start()
    barrier = pltpu.get_barrier_semaphore()
    peers = [(step, flip) for step in range(owners - 1, -1, -1) for flip in (0, 1) if step + flip]

    def peer_id(step, flip):
        return {"docs": flipped(me, step), "help": flipped(side, flip)}

    inner = [(spot, spot_side) for spot in range(quarter, half) for spot_side in (0, 1)]

    def greet(semaphore):
        def signal(spot, spot_side):
            docs = spot + my_half * (owners - 1 - 2 * spot)
            pl.semaphore_signal(
                semaphore,
                inc=1,
                device_id={"docs": docs, "help": spot_side},
                device_id_type=pl.DeviceIdType.MESH,
            )

        @pl.when(is_owner)
        def _():
            for spot, spot_side in inner:
                signal(owners - 1 - spot, spot_side)
                signal(spot - quarter, spot_side)

        @pl.when(jnp.logical_not(is_owner))
        def _():
            for spot, spot_side in inner:
                signal(spot, spot_side)

    def await_greetings(semaphore):
        pl.semaphore_wait(semaphore, len(inner) * (2 - outer))

    greet(barrier)

    ids = ids_ref[...]
    across = jnp.broadcast_to(ids, (row_count, row_count))
    down = jnp.transpose(across)
    earlier = lax.broadcasted_iota(jnp.int32, (row_count, row_count), 0) < lax.broadcasted_iota(
        jnp.int32, (row_count, row_count), 1
    )
    rank = jnp.sum(jnp.where((across == down) & earlier, 1, 0), axis=0, keepdims=True)
    dest = ids // CL_OWN

    counts = jnp.transpose(
        jnp.broadcast_to(lengths_ref[...].astype(jnp.float32), (row_count, row_count))
    )[:, 0:1]
    states_copy.wait()
    states = states_ref[...]
    summed = states[:, 0, :].astype(jnp.float32)
    for position in range(1, seq_len):
        token = states[:, position, :].astype(jnp.float32)
        summed = summed + jnp.where(counts > position, token, 0.0)
    pooled = (summed / counts).astype(jnp.bfloat16)

    weight_copy.wait()
    hidden = jnp.tanh(
        jnp.dot(pooled, weight_ref[...], preferred_element_type=jnp.float32) + bias_ref[...]
    )
    factor = lax.rsqrt(jnp.sum(hidden * hidden, axis=1, keepdims=True) + 1e-06)
    embedded = (hidden * factor).astype(jnp.bfloat16)

    def turn_target(turn):
        spot = quarter + (turn // 2 + (1 - outer) * quarter) % half
        spot_side = turn % 2
        docs = spot + my_half * (owners - 1 - 2 * spot)
        number = (docs - quarter) * 2 + spot_side
        crosses = spot // half
        slot = (near + crosses * (owners - 1 - 2 * near)) * 2 + side
        return docs, spot_side, number, slot

    def pack(number):
        slots = lax.broadcasted_iota(jnp.int32, (slot_cap, row_count), 0)
        chooser = jnp.where((slots == rank) & (dest == number), 1.0, 0.0)
        filled = jnp.sum(chooser, axis=1, keepdims=True)
        rows = jnp.dot(
            chooser.astype(jnp.bfloat16), embedded, preferred_element_type=jnp.float32
        )
        return jnp.where(filled > 0.5, rows, EMPTY).astype(jnp.bfloat16)

    def to_owner(turn):
        docs, spot_side, _, slot = turn_target(turn)
        return pltpu.make_async_remote_copy(
            src_ref=packed_ref.at[turn],
            dst_ref=own_ref.at[slot],
            send_sem=pack_send.at[turn],
            recv_sem=pack_recv.at[slot],
            device_id={"docs": docs, "help": spot_side},
            device_id_type=pl.DeviceIdType.MESH,
        )

    def from_source(slot):
        return pltpu.make_async_remote_copy(
            src_ref=packed_ref.at[0],
            dst_ref=own_ref.at[slot],
            send_sem=pack_send.at[0],
            recv_sem=pack_recv.at[slot],
            device_id=peer_id(0, 1),
            device_id_type=pl.DeviceIdType.MESH,
        )

    my_number = (me - quarter) * 2 + side
    my_slot = near * 2 + side

    def back(number, position):
        where = peer_id(*peers[position])
        slot = (where["docs"] + my_half * (owners - 1 - 2 * where["docs"])) * 2 + where["help"]
        return pltpu.make_async_remote_copy(
            src_ref=maxima_ref.at[slot // group],
            dst_ref=returned_ref.at[number],
            send_sem=back_send.at[position],
            recv_sem=back_recv.at[number],
            device_id=where,
            device_id_type=pl.DeviceIdType.MESH,
        )

    for turn in range(owners):
        docs, spot_side, number, slot = turn_target(turn)
        remote = (docs != me) | (side != spot_side)
        packed_ref[turn] = pack(number)
        if turn == 0:
            await_greetings(barrier)
            greet(onward_sem)
        if turn == half:
            await_greetings(onward_sem)

        @pl.when(remote)
        def _():
            to_owner(turn).start()

        @pl.when(jnp.logical_not(remote))
        def _():
            own_ref[slot] = packed_ref[turn]

    def column_max(columns, rows, same):
        scores = lax.dot_general(
            columns, rows, (((1,), (1,)), ((), ())), preferred_element_type=jnp.float32
        )
        keep = columns[:, 0:1].astype(jnp.float32) < 1.5
        if same:
            keep = keep & (
                lax.broadcasted_iota(jnp.int32, scores.shape, 0)
                != lax.broadcasted_iota(jnp.int32, scores.shape, 1)
            )
        return jnp.max(jnp.where(keep, scores, -1.0), axis=0, keepdims=True)

    @pl.when(is_owner)
    def _():
        for slot in range(late):

            @pl.when(my_slot != slot)
            def _():
                from_source(slot).wait_recv()

        first = own_ref[:late].reshape(late * slot_cap, feat_dim)
        first_max = column_max(first, first, True)
        for slot in range(late, sources):
            from_source(slot).wait_recv()
        last = own_ref[late:].reshape((sources - late) * slot_cap, feat_dim)
        maxima = jnp.concatenate(
            [
                jnp.maximum(first_max, column_max(last, first, False)),
                jnp.maximum(column_max(first, last, False), column_max(last, last, True)),
            ],
            axis=1,
        )
        for part in range(sources // group):
            maxima_ref[part] = maxima[:, part * row_count : (part + 1) * row_count]
        for position in range(len(peers)):
            back(my_number, position).start()
        returned_ref[my_number] = maxima_ref[my_slot // group]

    owner_half = (dest // 2 + quarter) // half
    my_slots = jnp.where(owner_half == my_half, near, owners - 1 - near) * 2 + side
    finder = jnp.where(
        lax.broadcasted_iota(jnp.int32, (row_count, row_count), 0)
        == my_slots % group * slot_cap + rank,
        1.0,
        0.0,
    ).astype(jnp.bfloat16)
    for number in range(owners):

        @pl.when((my_number != number) | jnp.logical_not(is_owner))
        def _():
            back(number, 0).wait_recv()

    exact = jnp.concatenate([returned_ref[number] for number in range(owners)], axis=0)
    parts = []
    for _ in range(3):
        part = exact.astype(jnp.bfloat16)
        parts.append(part.astype(jnp.float32))
        exact = exact - parts[-1]
    picked = jnp.dot(
        jnp.concatenate(parts, axis=0).astype(jnp.bfloat16),
        finder,
        preferred_element_type=jnp.float32,
    )
    picked = picked[:owners] + (picked[owners : 2 * owners] + picked[2 * owners :])
    mine = lax.broadcasted_iota(jnp.int32, picked.shape, 0) == dest
    out_ref[...] = jnp.sum(jnp.where(mine, picked, 0.0), axis=0, keepdims=True)
    for turn in range(owners):
        docs, spot_side, _, _ = turn_target(turn)

        @pl.when((docs != me) | (side != spot_side))
        def _():
            to_owner(turn).wait_send()

    @pl.when(is_owner)
    def _():
        for position in range(len(peers)):
            back(my_number, position).wait_send()


def fused_body(token_states, lengths, cluster_id, proj_weight, proj_bias):
    row_count, seq_len, feat_dim = token_states.shape
    owners = lax.axis_size("docs")
    slot_cap = 2 * row_count // owners
    vmem = pl.BlockSpec(memory_space=pltpu.VMEM)
    hbm = pl.BlockSpec(memory_space=pl.ANY)
    sources = 2 * owners
    result = pl.pallas_call(
        functools.partial(fused_kernel, owners, slot_cap),
        out_shape=jax.ShapeDtypeStruct((1, row_count), jnp.float32),
        in_specs=[hbm, vmem, vmem, hbm, vmem],
        out_specs=vmem,
        scratch_shapes=[
            pltpu.VMEM(token_states.shape, jnp.bfloat16),
            pltpu.VMEM(proj_weight.shape, jnp.bfloat16),
            pltpu.VMEM((owners, slot_cap, feat_dim), jnp.bfloat16),
            pltpu.VMEM((sources, slot_cap, feat_dim), jnp.bfloat16),
            pltpu.VMEM((sources * slot_cap // row_count, 1, row_count), jnp.float32),
            pltpu.VMEM((owners, 1, row_count), jnp.float32),
            pltpu.SemaphoreType.DMA,
            pltpu.SemaphoreType.DMA,
            pltpu.SemaphoreType.DMA((owners,)),
            pltpu.SemaphoreType.DMA((sources,)),
            pltpu.SemaphoreType.DMA((sources,)),
            pltpu.SemaphoreType.DMA((owners,)),
            pltpu.SemaphoreType.REGULAR,
        ],
        compiler_params=pltpu.CompilerParams(collective_id=0, has_side_effects=True),
        name="scores",
    )(token_states, lengths[None, :], cluster_id[None, :], proj_weight, proj_bias[None, :])
    return result.reshape(row_count)


def solution(mesh):
    in_specs = (
        P(("groups", "docs", "help"), None, None),
        P(("groups", "docs", "help")),
        P(("groups", "docs", "help")),
        P(),
        P(),
    )
    out_specs = P(("groups", "docs", "help"))
    owners = mesh.shape["docs"]
    direct = 8 <= owners <= DIRECT_LIMIT and owners & (owners - 1) == 0 and mesh.shape["help"] == 2
    return jax.shard_map(fused_body if direct else body, mesh=mesh, in_specs=in_specs, out_specs=out_specs, check_vma=False)
```

time: 26.5 us -> 25.9 us (0.977)
  Pallas kernels: 25 us -> 24.5 us
    pallas_call x1, Pallas kernels: 25 us -> 24.5 us  [fused_body(): pl.pallas_call(functools.partial(fused_kernel, owners, slot_cap), out_sha...]
where the time goes in v3:
time: 25.9 us; the launch traced here: 25.7 us
  Pallas kernels  24.5 us (95%)
  local copies, waits for them, and re-layouts  1.19 us (5%)
    pallas_call x1, Pallas kernels, fused_body(): pl.pallas_call(functools.partial(fused_kernel, owners, slot_cap), out_sha...  24.5 us
    unnamed x1, local copies, waits for them, and re-layouts  1.19 us

profile of v3, /device:TPU:0, one launch (start us, length us, event | category | flops | bytes accessed | tf_op | source)
XLA Modules:
  0.0 25.7 jit_solution(7360041149792778830)
XLA Ops:
  0.0 24.5 %scores.1 = f32[1,128]{1,0:T(1,128)} custom-call(bf16[128,2,1024]{2,1,0:T(2,128)(2,1)} %states_hbm.1, s32[1,128]{1,0:T(1,128)} %bitcast.5, s32[1,128]{1,0:T(1,128)} %bitcast.6, bf16[1024,1024]{1,0:T(8,128)(2,1)} %weight_hbm.1, f32[1,1024]{1,0:T(1,128)} %bitcast.4), custom_call_target="tpu_custom_call" | custom-call | tf_op jit(solution)/shard_map/scores/pallas_call | solution.py:356
  24.5 1.2 %copy.7 = f32[128]{0:T(128)} copy(f32[128]{0:T(128)} %bitcast.7) | data formatting | bytes 1024

commit v4 on v3

--- a/solution.py
+++ b/solution.py
@@ -98,17 +98,21 @@
     owners,
     slot_cap,
     states_hbm,
+    lengths_hbm,
+    ids_hbm,
+    weight_hbm,
+    bias_hbm,
+    out_ref,
     lengths_ref,
     ids_ref,
-    weight_hbm,
     bias_ref,
-    out_ref,
     states_ref,
     weight_ref,
     packed_ref,
     own_ref,
     maxima_ref,
     returned_ref,
+    small_sem,
     states_sem,
     weight_sem,
     pack_send,
@@ -130,6 +134,14 @@
     outer = 1 - near // quarter
     is_owner = near >= quarter
 
+    small_copies = [
+        pltpu.make_async_copy(source, held, small_sem.at[position])
+        for position, (source, held) in enumerate(
+            [(ids_hbm, ids_ref), (lengths_hbm, lengths_ref), (bias_hbm, bias_ref)]
+        )
+    ]
+    for copy in small_copies:
+        copy.start()
     states_copy = pltpu.make_async_copy(states_hbm, states_ref, states_sem)
     states_copy.start()
     weight_copy = pltpu.make_async_copy(weight_hbm, weight_ref, weight_sem)
@@ -168,6 +180,8 @@
 
     greet(barrier)
 
+    for copy in small_copies:
+        copy.wait()
     ids = ids_ref[...]
     across = jnp.broadcast_to(ids, (row_count, row_count))
     down = jnp.transpose(across)
@@ -355,16 +369,20 @@
     sources = 2 * owners
     result = pl.pallas_call(
         functools.partial(fused_kernel, owners, slot_cap),
-        out_shape=jax.ShapeDtypeStruct((1, row_count), jnp.float32),
-        in_specs=[hbm, vmem, vmem, hbm, vmem],
+        out_shape=pltpu.VMEM((1, row_count), jnp.float32),
+        in_specs=[hbm] * 5,
         out_specs=vmem,
         scratch_shapes=[
+            pltpu.VMEM((1, row_count), jnp.int32),
+            pltpu.VMEM((1, row_count), jnp.int32),
+            pltpu.VMEM((1, feat_dim), jnp.float32),
             pltpu.VMEM(token_states.shape, jnp.bfloat16),
             pltpu.VMEM(proj_weight.shape, jnp.bfloat16),
             pltpu.VMEM((owners, slot_cap, feat_dim), jnp.bfloat16),
             pltpu.VMEM((sources, slot_cap, feat_dim), jnp.bfloat16),
             pltpu.VMEM((sources * slot_cap // row_count, 1, row_count), jnp.float32),
             pltpu.VMEM((owners, 1, row_count), jnp.float32),
+            pltpu.SemaphoreType.DMA((3,)),
             pltpu.SemaphoreType.DMA,
             pltpu.SemaphoreType.DMA,
             pltpu.SemaphoreType.DMA((owners,)),

time: 25.9 us -> 24 us (0.927)
  Pallas kernels: 24.5 us -> 23.3 us
  local copies, waits for them, and re-layouts: 1.19 us -> 0.51 us
    pallas_call x1, Pallas kernels: 24.5 us -> 23.3 us  [fused_body(): pl.pallas_call(functools.partial(fused_kernel, owners, slot_cap), out_sha...]
    unnamed x1, local copies, waits for them, and re-layouts: 1.19 us -> 0.51 us
where the time goes in v4:
time: 24 us; the launch traced here: 23.8 us
  Pallas kernels  23.3 us (97%)
  local copies, waits for them, and re-layouts  0.51 us (2%)
    pallas_call x1, Pallas kernels, fused_body(): pl.pallas_call(functools.partial(fused_kernel, owners, slot_cap), out_sha...  23.3 us
    unnamed x1, local copies, waits for them, and re-layouts  0.51 us

profile of v4, /device:TPU:0, one launch (start us, length us, event | category | flops | bytes accessed | tf_op | source)
XLA Modules:
  0.0 23.8 jit_solution(9779230562354723585)
XLA Ops:
  0.0 23.3 %scores.1 = f32[1,128]{1,0:T(1,128)S(1)} custom-call(bf16[128,2,1024]{2,1,0:T(2,128)(2,1)} %states_hbm.1, s32[1,128]{1,0:T(1,128)} %bitcast.6, s32[1,128]{1,0:T(1,128)} %bitcast.7, bf16[1024,1024]{1,0:T(8,128)(2,1)} %weight_hbm.1, f32[1,1024]{1,0:T(1,128)} %bitcast.5), custom_call_target="tpu_custom_call" | custom-call | tf_op jit(solution)/shard_map/scores/pallas_call | solution.py:370
  23.3 0.5 %copy.7 = f32[128]{0:T(128)} copy(f32[128]{0:T(128)S(1)} %bitcast.4) | data formatting | bytes 1024
